TPU v7x, 128 devices: a whole 4x4x4 slice. The times are simulated.
128 devices in a mesh: dp: 16 (over x, z), tensor: 8 (over y, core).
Axes of the slice: x: 4, y: 4, z: 4, core: 2. Of those that a mesh axis runs over, the one named last changes fastest.
Arguments:
- attn_norm_grad: bfloat16 [16, 2048], P('dp', 'tensor'), may hold values from -1.5 to 1.5
- query_grad: bfloat16 [16, 2048, 2048], P('dp', None, 'tensor'), may hold values from -1.5 to 1.5
- forget_grad: bfloat16 [16, 2048, 2048], P('dp', None, 'tensor'), may hold values from -1.5 to 1.5
- input_grad: bfloat16 [16, 2048, 2048], P('dp', None, 'tensor'), may hold values from -1.5 to 1.5
- group_norm_grad: bfloat16 [16, 2048], P('dp', 'tensor'), may hold values from -1.5 to 1.5
- output_gate_grad: bfloat16 [16, 2048, 2048], P('dp', None, 'tensor'), may hold values from -1.5 to 1.5
- out_proj_grad: bfloat16 [16, 2048, 2048], P('dp', 'tensor'), may hold values from -1.5 to 1.5
- mlp_norm_grad: bfloat16 [16, 2048], P('dp', 'tensor'), may hold values from -1.5 to 1.5
- gate_proj_grad: bfloat16 [16, 2048, 2816], P('dp', None, 'tensor'), may hold values from -1.5 to 1.5
- up_proj_grad: bfloat16 [16, 2048, 2816], P('dp', None, 'tensor'), may hold values from -1.5 to 1.5
- down_proj_grad: bfloat16 [16, 2816, 2048], P('dp', 'tensor'), may hold values from -1.5 to 1.5
- weights: float32 [8, 4784896], P('tensor', 'dp'), as said below
- first_moment: float32 [8, 4784896], P('tensor', 'dp'), may hold values from -0.6 to 0.6
- second_moment: float32 [8, 4784896], P('tensor', 'dp'), may hold values from 0.001 to 1
Outputs:
- new_weights: float32 [8, 4784896], P('tensor', 'dp')
- new_first: float32 [8, 4784896], P('tensor', 'dp')
- new_second: float32 [8, 4784896], P('tensor', 'dp')
- attn_norm_copy: bfloat16 [2048], P('tensor')
- query_copy: bfloat16 [2048, 2048], P(None, 'tensor')
- forget_copy: bfloat16 [2048, 2048], P(None, 'tensor')
- input_copy: bfloat16 [2048, 2048], P(None, 'tensor')
- group_norm_copy: bfloat16 [2048], P('tensor')
- output_gate_copy: bfloat16 [2048, 2048], P(None, 'tensor')
- out_proj_copy: bfloat16 [2048, 2048], P('tensor')
- mlp_norm_copy: bfloat16 [2048], P('tensor')
- gate_proj_copy: bfloat16 [2048, 2816], P(None, 'tensor')
- up_proj_copy: bfloat16 [2048, 2816], P(None, 'tensor')
- down_proj_copy: bfloat16 [2816, 2048], P('tensor')
Inputs may be any that keep to these rules, and one draw needn't show every extreme that they name: float32 master weights of order one.
All inputs are finite; a program needn't handle non-finite values.
Results may differ from a plain program's by a relative error of at most 0.0085.
Values may be sent and summed in bfloat16 or wider, within the bound.
A program may use at most 192 MiB of HBM per device.

v0:
```python
import jax
import jax.numpy as jnp
from jax import lax
from jax.sharding import PartitionSpec as P

GAIN_SEGMENTS = (0, 4, 7)


def segment_sums(onehot, values):
    return jnp.dot(onehot, values, precision=lax.Precision.HIGHEST)


def split_rows(block, owners):
    if block.ndim == 1:
        return block.reshape(owners, block.shape[0] // owners)
    return block.reshape(owners, block.shape[0] // owners, block.shape[1])


def on_device(
    attn_norm_grad,
    query_grad,
    forget_grad,
    input_grad,
    group_norm_grad,
    output_gate_grad,
    out_proj_grad,
    mlp_norm_grad,
    gate_proj_grad,
    up_proj_grad,
    down_proj_grad,
    weights,
    first_moment,
    second_moment,
):
    grads = (
        attn_norm_grad,
        query_grad,
        forget_grad,
        input_grad,
        group_norm_grad,
        output_gate_grad,
        out_proj_grad,
        mlp_norm_grad,
        gate_proj_grad,
        up_proj_grad,
        down_proj_grad,
    )
    owners = lax.axis_size("dp")
    shapes = [g.shape[1:] for g in grads]
    pieces = [split_rows(g[0], owners) for g in grads]
    piece_len = [p[0].size for p in pieces]
    own_count = sum(piece_len)
    weight_row = weights.reshape(-1)
    first_row = first_moment.reshape(-1)
    second_row = second_moment.reshape(-1)
    position = jnp.arange(own_count, dtype=jnp.int32)
    segment = jnp.zeros((own_count,), jnp.int32)
    bound = 0
    for number in range(10):
        bound += piece_len[number]
        segment = segment + (position >= bound).astype(jnp.int32)
    onehot = (segment[None, :] == jnp.arange(11, dtype=jnp.int32)[:, None]).astype(jnp.float32)
    gain_mask = onehot[GAIN_SEGMENTS[0]] + onehot[GAIN_SEGMENTS[1]] + onehot[GAIN_SEGMENTS[2]]
    summed = (
        lax.psum_scatter(
            pieces[0].astype(jnp.float32).astype(jnp.bfloat16),
            "dp",
            scatter_dimension=0,
            tiled=True,
        ).astype(jnp.float32),
        lax.psum_scatter(
            pieces[1].astype(jnp.float32).astype(jnp.bfloat16),
            "dp",
            scatter_dimension=0,
            tiled=True,
        ).astype(jnp.float32),
        lax.psum_scatter(
            pieces[2].astype(jnp.float32).astype(jnp.bfloat16),
            "dp",
            scatter_dimension=0,
            tiled=True,
        ).astype(jnp.float32),
        lax.psum_scatter(
            pieces[3].astype(jnp.float32).astype(jnp.bfloat16),
            "dp",
            scatter_dimension=0,
            tiled=True,
        ).astype(jnp.float32),
        lax.psum_scatter(
            pieces[4].astype(jnp.float32).astype(jnp.bfloat16),
            "dp",
            scatter_dimension=0,
            tiled=True,
        ).astype(jnp.float32),
        lax.psum_scatter(
            pieces[5].astype(jnp.float32).astype(jnp.bfloat16),
            "dp",
            scatter_dimension=0,
            tiled=True,
        ).astype(jnp.float32),
        lax.psum_scatter(
            pieces[6].astype(jnp.float32).astype(jnp.bfloat16),
            "dp",
            scatter_dimension=0,
            tiled=True,
        ).astype(jnp.float32),
        lax.psum_scatter(
            pieces[7].astype(jnp.float32).astype(jnp.bfloat16),
            "dp",
            scatter_dimension=0,
            tiled=True,
        ).astype(jnp.float32),
        lax.psum_scatter(
            pieces[8].astype(jnp.float32).astype(jnp.bfloat16),
            "dp",
            scatter_dimension=0,
            tiled=True,
        ).astype(jnp.float32),
        lax.psum_scatter(
            pieces[9].astype(jnp.float32).astype(jnp.bfloat16),
            "dp",
            scatter_dimension=0,
            tiled=True,
        ).astype(jnp.float32),
        lax.psum_scatter(
            pieces[10].astype(jnp.float32).astype(jnp.bfloat16),
            "dp",
            scatter_dimension=0,
            tiled=True,
        ).astype(jnp.float32),
    )
    grad = jnp.concatenate([s.reshape(-1) for s in summed])
    new_first = 0.9 * first_row + 0.1 * grad
    new_second = 0.999 * second_row + 0.001 * grad * grad
    update = new_first / (jnp.sqrt(new_second) + 1e-06) + 0.01 * weight_row * (1.0 - gain_mask)
    weight_sq, update_sq = lax.psum(
        (segment_sums(onehot, weight_row * weight_row), segment_sums(onehot, update * update)),
        ("dp", "tensor"),
    )
    trust = jnp.sqrt(weight_sq) / jnp.sqrt(update_sq)
    scale = jnp.dot(trust, onehot, precision=lax.Precision.HIGHEST)
    new_weights = weight_row - 0.1 * scale * update
    rounded = new_weights.astype(jnp.bfloat16)
    owned = []
    offset = 0
    for number in range(11):
        owned.append(
            rounded[offset : offset + piece_len[number]].reshape((1,) + pieces[number].shape[1:])
        )
        offset += piece_len[number]
    gathered = (
        lax.all_gather(owned[0], "dp", axis=0, tiled=True),
        lax.all_gather(owned[1], "dp", axis=0, tiled=True),
        lax.all_gather(owned[2], "dp", axis=0, tiled=True),
        lax.all_gather(owned[3], "dp", axis=0, tiled=True),
        lax.all_gather(owned[4], "dp", axis=0, tiled=True),
        lax.all_gather(owned[5], "dp", axis=0, tiled=True),
        lax.all_gather(owned[6], "dp", axis=0, tiled=True),
        lax.all_gather(owned[7], "dp", axis=0, tiled=True),
        lax.all_gather(owned[8], "dp", axis=0, tiled=True),
        lax.all_gather(owned[9], "dp", axis=0, tiled=True),
        lax.all_gather(owned[10], "dp", axis=0, tiled=True),
    )
    copies = [gathered[number].reshape(shapes[number]) for number in range(11)]
    return (
        new_weights.reshape(1, -1),
        new_first.reshape(1, -1),
        new_second.reshape(1, -1),
        copies[0],
        copies[1],
        copies[2],
        copies[3],
        copies[4],
        copies[5],
        copies[6],
        copies[7],
        copies[8],
        copies[9],
        copies[10],
    )


def solution(mesh):
    return jax.shard_map(
        on_device,
        mesh=mesh,
        in_specs=(
            P("dp", "tensor"),
            P("dp", None, "tensor"),
            P("dp", None, "tensor"),
            P("dp", None, "tensor"),
            P("dp", "tensor"),
            P("dp", None, "tensor"),
            P("dp", "tensor", None),
            P("dp", "tensor"),
            P("dp", None, "tensor"),
            P("dp", None, "tensor"),
            P("dp", "tensor", None),
            P("tensor", "dp"),
            P("tensor", "dp"),
            P("tensor", "dp"),
        ),
        out_specs=(
            P("tensor", "dp"),
            P("tensor", "dp"),
            P("tensor", "dp"),
            P("tensor"),
            P(None, "tensor"),
            P(None, "tensor"),
            P(None, "tensor"),
            P("tensor"),
            P(None, "tensor"),
            P("tensor", None),
            P("tensor"),
            P(None, "tensor"),
            P(None, "tensor"),
            P("tensor", None),
        ),
        check_vma=False,
    )
```

profile of v0, /device:TPU:0, one launch (start us, length us, event | category | flops | bytes accessed | tf_op | source)
XLA Modules:
  0.0 1172.6 jit_solution(3635013927501478566)
XLA Ops:
  11.1 1.5 copy.40
  12.7 1.3 copy-done.2
  14.3 1.5 copy.42
  15.9 1.3 copy-done.3
  17.2 1.4 reshape_squeeze.43
  18.8 8.6 fusion.2
  27.7 13.4 %reduce = f32[299056]{0:T(1024)S(1)} reduce(f32[1,299056]{1,0:T(1,128)} %param.25, f32[]{:T(128)} %constant.110), dimensions={0}, to_apply=%param.25.reduce_sub_computation | reduce | bytes 2392452 | tf_op args[11]
  41.1 76.1 %all-reduce.16 = (bf16[16,16]{1,0:T(8,128)(2,1)S(1)}, bf16[16,16]{1,0:T(8,128)(2,1)S(1)}, bf16[16,16]{1,0:T(8,128)(2,1)S(1)}) all-reduce(bf16[16,16]{1,0:T(8,128)(2,1)S(1)} %reshape_squeeze.33, bf16[16,16]{1,0:T(8,128)(2,1)S(1)} %reshape_squeeze.37, ...), channel_id=5, replica_groups=mesh['dp'=16,'tensor'=8] {'dp'}, use_global_device_ids=true, to_apply=%region_1.0.clone | all-reduce | flops 768 | bytes 3072
  119.1 1.2 dynamic-update-slice.3
  121.0 20.0 %fusion.15 = f32[299056]{0:T(1024)} fusion(f32[11,299056]{1,0:T(8,128)} %fusion.2), kind=kLoop, calls=%fused_computation.35 | loop fusion | flops 897168 | bytes 4784896 | tf_op jit(solution)/shard_map/sub | solution.py:135
  141.0 0.9 convert_bitcast_fusion.8
  142.1 20.7 %reduce-scatter.27.cloned.1.call-done = bf16[1,128,256]{2,1,0:T(8,128)(2,1)} async-done(((bf16[16,128,256]{2,1,0:T(8,128)(2,1)}), bf16[1,128,256]{2,1,0:T(8,128)(2,1)}) %reduce-scatter.27.cloned.1.call-update) | async-done | bytes 65552
  162.7 0.9 convert_bitcast_fusion.6
  163.7 74.5 %reduce-scatter.29.cloned.1.call-done = bf16[1,128,256]{2,1,0:T(8,128)(2,1)} async-done(((bf16[16,128,256]{2,1,0:T(8,128)(2,1)}), bf16[1,128,256]{2,1,0:T(8,128)(2,1)}) %reduce-scatter.29.cloned.1.call-update) | async-done | bytes 65552
  238.3 1.5 convert_bitcast_fusion.4
  239.9 74.0 %reduce-scatter.31.cloned.1.call-done = bf16[1,128,256]{2,1,0:T(8,128)(2,1)} async-done(((bf16[16,128,256]{2,1,0:T(8,128)(2,1)}), bf16[1,128,256]{2,1,0:T(8,128)(2,1)}) %reduce-scatter.31.cloned.1.call-update) | async-done | bytes 65552
  313.9 1.5 convert_bitcast_fusion.2
  315.6 73.7 %reduce-scatter.33.cloned.1.call-done = bf16[1,16,2048]{2,1,0:T(8,128)(2,1)} async-done(((bf16[16,16,2048]{2,1,0:T(8,128)(2,1)}), bf16[1,16,2048]{2,1,0:T(8,128)(2,1)}) %reduce-scatter.33.cloned.1.call-update) | async-done | bytes 65552
  389.3 0.9 convert_bitcast_fusion
  390.5 0.7 copy.53
  393.3 3.8 dynamic-update-slice.4
  397.1 3.8 dynamic-update-slice.5
  400.8 3.8 dynamic-update-slice.6
  404.6 1.4 dynamic-update-slice.7
  405.9 3.8 dynamic-update-slice.8
  409.7 3.8 dynamic-update-slice.9
  413.5 1.4 dynamic-update-slice.10
  414.8 51.4 %reduce-scatter.35.cloned.1.call-done = bf16[1,128,352]{1,2,0:T(8,128)(2,1)} async-done(((bf16[16,128,352]{1,2,0:T(8,128)(2,1)}), bf16[1,128,352]{1,2,0:T(8,128)(2,1)}) %reduce-scatter.35.cloned.1.call-update) | async-done | bytes 90128
  466.2 1.0 copy.41
  467.7 75.6 %reduce-scatter.37.cloned.1.call-done = bf16[1,128,352]{1,2,0:T(8,128)(2,1)} async-done(((bf16[16,128,352]{1,2,0:T(8,128)(2,1)}), bf16[1,128,352]{1,2,0:T(8,128)(2,1)}) %reduce-scatter.37.cloned.1.call-update) | async-done | bytes 90128
  543.3 1.0 copy.43
  544.8 75.0 %reduce-scatter.39.cloned.1.call-done = bf16[1,22,2048]{2,1,0:T(8,128)(2,1)} async-done(((bf16[16,22,2048]{2,1,0:T(8,128)(2,1)}), bf16[1,22,2048]{2,1,0:T(8,128)(2,1)}) %reduce-scatter.39.cloned.1.call-update) | async-done | bytes 90128
  619.8 0.9 convert_bitcast_fusion.10
  620.9 4.4 dynamic-update-slice.11
  625.3 4.4 dynamic-update-slice.12
  629.6 4.3 dynamic-update-slice.13
  634.0 21.6 %fusion.13 = (f32[1,299056]{1,0:T(1,128)}, f32[299056]{0:T(1024)}, f32[1,299056]{1,0:T(1,128)}, f32[299056]{0:T(1024)}) fusion(f32[1,299056]{1,0:T(1,128)} %dynamic-update-slice.13, f32[1,299056]{1,0:T(1,128)} %param.27, f32[1,299056]{1,0:T(1,128)} %param.26), kind=kLoop, calls=%fused_computation.30 | loop fusion | flops 2093392 | bytes 8373568 | tf_op jit(solution)/shard_map/add | solution.py:134
  655.7 16.2 %concatenate.41 = f32[299056]{0:T(1024)} concatenate(f32[16]{0:T(128)S(1)} %bitcast.103, f32[32768]{0:T(1024)S(1)} %bitcast.93, f32[32768]{0:T(1024)S(1)} %bitcast.94, f32[32768]{0:T(1024)S(1)} %bitcast.95, f32[16]{0:T(128)S(1)} %fusion.32, f32[32768]{0:T(1024)} %bitcast.96, f32[32768]{0:T(1024)} %bitcast.97, f32[16]{0:T(128)S(1)} %bitcast.104, f32[45056]{0:T(1024)S(1)} %reshape.617, ...), dimensions={0} | concatenate | bytes 2392448 | tf_op jit(solution)/shard_map/concatenate | solution.py:132
  671.9 4.2 fusion.24
  676.1 5.7 reshape.666
  681.8 12.5 %fusion.17 = f32[11]{0:T(128)S(1)} fusion(f32[299056,1]{0,1:T(1,128)S(1)} %reshape.666, s32[299056]{0:T(1024)S(1)} %convert_add_fusion), kind=kOutput, calls=%fused_computation.37 | convolution fusion | flops 42765008 | bytes 2392492 | tf_op jit(solution)/shard_map/dot_general | solution.py:10
  694.3 5.8 reshape.664
  700.1 12.5 %fusion.16 = f32[11]{0:T(128)S(1)} fusion(f32[299056,1]{0,1:T(1,128)S(1)} %reshape.664, s32[299056]{0:T(1024)S(1)} %convert_add_fusion), kind=kOutput, calls=%fused_computation.36 | convolution fusion | flops 42765008 | bytes 2392492 | tf_op jit(solution)/shard_map/dot_general | solution.py:10
  712.6 65.0 %all-reduce.14 = (f32[11]{0:T(128)S(1)}, f32[11]{0:T(128)S(1)}) all-reduce(f32[11]{0:T(128)S(1)} %fusion.17, f32[11]{0:T(128)S(1)} %fusion.16), channel_id=1, replica_groups=mesh['dp'=16,'tensor'=8] {'dp','tensor'}, use_global_device_ids=true, to_apply=%region_12.0 | all-reduce | flops 22 | bytes 176 | tf_op jit(solution)/shard_map/psum | solution.py:136
  777.6 20.0 %fusion.7 = f32[299056]{0:T(1024)S(1)} fusion(s32[299056]{0:T(1024)S(1)} %convert_add_fusion, f32[11]{0:T(128)S(1)} %get-tuple-element.28, f32[11]{0:T(128)S(1)} %get-tuple-element.29), kind=kOutput, calls=%fused_computation.22 | convolution fusion | flops 42765020 | bytes 2392536 | tf_op jit(solution)/shard_map/dot_general | solution.py:141
  802.0 0.7 copy.46
  803.0 0.7 copy.48
  805.2 6.5 reshape.620
  812.4 38.4 %all-reduce.15 = (bf16[256]{0:T(256)(128)(2,1)}, bf16[256]{0:T(256)(128)(2,1)}, bf16[256]{0:T(256)(128)(2,1)}) all-reduce(bf16[256]{0:T(256)(128)(2,1)S(1)} %dynamic-update-slice, bf16[256]{0:T(256)(128)(2,1)S(1)} %dynamic-update-slice.1, bf16[256]{0:T(256)(128)(2,1)S(1)} %dynamic-update-slice.2), channel_id=2, replica_groups=mesh['dp'=16,'tensor'=8] {'dp'}, use_global_device_ids=true, to_apply=%add | all-reduce | flops 768 | bytes 3072
  850.8 31.7 %all-gather.14.cloned.1.call-done = bf16[16,128,256]{2,1,0:T(8,128)(2,1)} async-done(((bf16[1,128,256]{2,1,0:T(8,128)(2,1)}), bf16[16,128,256]{2,1,0:T(8,128)(2,1)}) %all-gather.14.cloned.1.call-update) | async-done | bytes 1048592 | tf_op jit(solution)/shard_map/all_gather | solution.py:154
  882.5 45.1 %all-gather.16.cloned.1.call-done = bf16[16,128,256]{2,1,0:T(8,128)(2,1)} async-done(((bf16[1,128,256]{2,1,0:T(8,128)(2,1)}), bf16[16,128,256]{2,1,0:T(8,128)(2,1)}) %all-gather.16.cloned.1.call-update) | async-done | bytes 1048592 | tf_op jit(solution)/shard_map/all_gather | solution.py:155
  927.6 44.9 %all-gather.18.cloned.1.call-done = bf16[16,128,256]{2,1,0:T(8,128)(2,1)} async-done(((bf16[1,128,256]{2,1,0:T(8,128)(2,1)}), bf16[16,128,256]{2,1,0:T(8,128)(2,1)}) %all-gather.18.cloned.1.call-update) | async-done | bytes 1048592 | tf_op jit(solution)/shard_map/all_gather | solution.py:157
  972.5 45.1 %all-gather.20.cloned.1.call-done = bf16[16,16,2048]{2,1,0:T(8,128)(2,1)} async-done(((bf16[1,16,2048]{2,1,0:T(8,128)(2,1)}), bf16[16,16,2048]{2,1,0:T(8,128)(2,1)}) %all-gather.20.cloned.1.call-update) | async-done | bytes 1048592 | tf_op jit(solution)/shard_map/all_gather | solution.py:158
  1017.6 46.1 %all-gather.22.cloned.1.call-done = bf16[16,128,352]{1,2,0:T(8,128)(2,1)} async-done(((bf16[1,128,352]{1,2,0:T(8,128)(2,1)}), bf16[16,128,352]{1,2,0:T(8,128)(2,1)}) %all-gather.22.cloned.1.call-update) | async-done | bytes 1441808 | tf_op jit(solution)/shard_map/all_gather | solution.py:160
  1063.7 2.6 copy_bitcast_fusion.1
  1066.3 43.5 %all-gather.24.cloned.1.call-done = bf16[16,128,352]{1,2,0:T(8,128)(2,1)} async-done(((bf16[1,128,352]{1,2,0:T(8,128)(2,1)}), bf16[16,128,352]{1,2,0:T(8,128)(2,1)}) %all-gather.24.cloned.1.call-update) | async-done | bytes 1441808 | tf_op jit(solution)/shard_map/all_gather | solution.py:161
  1109.8 2.6 copy_bitcast_fusion
  1112.4 43.6 %all-gather.26.cloned.1.call-done = bf16[16,22,2048]{2,1,0:T(8,128)(2,1)} async-done(((bf16[1,22,2048]{2,1,0:T(8,128)(2,1)}), bf16[16,22,2048]{2,1,0:T(8,128)(2,1)}) %all-gather.26.cloned.1.call-update) | async-done | bytes 1441808 | tf_op jit(solution)/shard_map/all_gather | solution.py:162
  1156.0 2.4 reshape.642
  1158.5 1.0 copy.86
  1160.1 1.0 copy.87
  1161.7 1.0 copy.88
  1163.3 1.0 copy.89
  1164.9 1.0 copy.90
  (115 shorter events, 19.9 us)
Async XLA Ops:
  7.2 133.9 %reduce-scatter.25.cloned.1.call-start = ((), (), s32[]{:S(2)}) async-start(), calls=%async_computation.16 | async-start | bytes 1114112
  7.9 154.8 %reduce-scatter.27.cloned.1.call-start = ((), (), s32[]{:S(2)}) async-start(), calls=%async_computation.17 | async-start | bytes 1114112
  8.7 229.6 %reduce-scatter.29.cloned.1.call-start = ((), (), s32[]{:S(2)}) async-start(), calls=%async_computation.18 | async-start | bytes 1114112
  9.4 1.4 copy-start.1
  9.4 304.5 %reduce-scatter.31.cloned.1.call-start = ((), (), s32[]{:S(2)}) async-start(), calls=%async_computation.19 | async-start | bytes 1114112
  10.0 379.3 %reduce-scatter.33.cloned.1.call-start = ((), (), s32[]{:S(2)}) async-start(), calls=%async_computation.20 | async-start | bytes 1114112
  10.6 455.7 %reduce-scatter.35.cloned.1.call-start = ((), (), s32[]{:S(2)}) async-start(), calls=%async_computation.21 | async-start | bytes 1531904
  12.6 1.4 copy-start.2
  12.6 530.7 %reduce-scatter.37.cloned.1.call-start = ((), (), s32[]{:S(2)}) async-start(), calls=%async_computation.22 | async-start | bytes 1531904
  15.8 1.4 copy-start.3
  15.8 604.0 %reduce-scatter.39.cloned.1.call-start = ((), (), s32[]{:S(2)}) async-start(), calls=%async_computation.23 | async-start | bytes 1671168
  18.6 832.3 %all-gather.12.cloned.1.call-start = ((), (), s32[]{:S(2)}) async-start(), calls=%async_computation.8 | async-start | bytes 1114112 | tf_op jit(solution)/shard_map/all_gather | solution.py:153
  18.7 8.6 copy-start.15
  18.7 8.7 copy-start.16
  18.7 8.8 copy-start.17
  27.7 89.5 %copy-start.14 = (u32[128]{0:T(128)S(1)}, u32[128]{0:T(128)}, u32[]{:S(2)}) copy-start(u32[128]{0:T(128)} %constant.50) | copy-start | bytes 1540
  389.3 1.9 copy-start.11
  389.3 2.6 copy-start.12
  633.9 21.6 %copy-start.13 = (bf16[1,22,2048]{2,1,0:T(8,128)(2,1)S(1)}, bf16[1,22,2048]{2,1,0:T(8,128)(2,1)}, u32[]{:S(2)}) copy-start(bf16[1,22,2048]{2,1,0:T(8,128)(2,1)} %reduce-scatter.39.cloned.1.call-done) | copy-start | bytes 270340
  633.9 21.7 %copy-start.9 = (f32[16,2,8,128]{3,1,2,0:T(2,128)S(1)}, f32[16,2,8,128]{3,1,2,0:T(2,128)}, u32[]{:S(2)}) copy-start(f32[16,2,8,128]{3,1,2,0:T(2,128)} %copy.53) | copy-start | bytes 393220
  634.0 21.7 %copy-start.10 = (f32[16,2,8,128]{3,1,2,0:T(2,128)S(1)}, f32[16,2,8,128]{3,1,2,0:T(2,128)}, u32[]{:S(2)}) copy-start(f32[16,2,8,128]{3,1,2,0:T(2,128)} %copy.54) | copy-start | bytes 393220
  777.6 20.0 %copy-start = (f32[299056]{0:T(1024)S(1)}, f32[299056]{0:T(1024)}, u32[]{:S(2)}) copy-start(f32[299056]{0:T(1024)} %get-tuple-element.39) | copy-start | bytes 3588676
  798.7 83.8 %all-gather.14.cloned.1.call-start = ((), (), s32[]{:S(2)}) async-start(), calls=%async_computation.9 | async-start | bytes 1114112 | tf_op jit(solution)/shard_map/all_gather | solution.py:154
  799.5 128.2 %all-gather.16.cloned.1.call-start = ((), (), s32[]{:S(2)}) async-start(), calls=%async_computation.10 | async-start | bytes 1114112 | tf_op jit(solution)/shard_map/all_gather | solution.py:155
  800.2 172.3 %all-gather.18.cloned.1.call-start = ((), (), s32[]{:S(2)}) async-start(), calls=%async_computation.11 | async-start | bytes 1114112 | tf_op jit(solution)/shard_map/all_gather | solution.py:157
  800.9 216.7 %all-gather.20.cloned.1.call-start = ((), (), s32[]{:S(2)}) async-start(), calls=%async_computation.12 | async-start | bytes 1114112 | tf_op jit(solution)/shard_map/all_gather | solution.py:158
  801.7 262.0 %all-gather.22.cloned.1.call-start = ((), (), s32[]{:S(2)}) async-start(), calls=%async_computation.13 | async-start | bytes 1531904 | tf_op jit(solution)/shard_map/all_gather | solution.py:160
  802.8 307.0 %all-gather.24.cloned.1.call-start = ((), (), s32[]{:S(2)}) async-start(), calls=%async_computation.14 | async-start | bytes 1531904 | tf_op jit(solution)/shard_map/all_gather | solution.py:161
  803.8 352.2 %all-gather.26.cloned.1.call-start = ((), (), s32[]{:S(2)}) async-start(), calls=%async_computation.15 | async-start | bytes 1671168 | tf_op jit(solution)/shard_map/all_gather | solution.py:162
  1112.4 46.0 %copy-start.4 = (bf16[16,128,256]{2,1,0:T(8,128)(2,1)S(1)}, bf16[16,128,256]{2,1,0:T(8,128)(2,1)}, u32[]{:S(2)}) copy-start(bf16[16,128,256]{2,1,0:T(8,128)(2,1)} %all-gather.12.cloned.1.call-done) | copy-start | bytes 3145732
  1158.5 1.6 copy-start.5
  1160.1 1.6 copy-start.6
  1161.7 1.6 copy-start.7
  1163.3 1.6 copy-start.8
Sparse Core Ops, SparseCore 0:
  11.2 75.6 reduce-scatter.24
  90.4 72.2 reduce-scatter.26
  165.9 72.2 reduce-scatter.28
  241.7 72.2 reduce-scatter.30
  317.0 72.2 reduce-scatter.32
  393.3 72.8 reduce-scatter.34
  470.4 72.9 reduce-scatter.36
  546.9 72.9 reduce-scatter.38
  798.8 38.8 all-gather.11
  840.6 41.9 all-gather.13
  885.5 42.0 all-gather.15
  930.4 42.0 all-gather.17
  975.5 42.0 all-gather.19
  1020.5 43.1 all-gather.21
  1066.5 43.2 all-gather.23
  1112.6 43.3 all-gather.25
where the time goes:
time: 1180 us; the launch traced here: 1170 us
  waiting for transfers between devices  748 us (63%)
  blocking collectives  180 us (15%)
  local copies, waits for them, and re-layouts  107 us (9%)
  other arithmetic  76.6 us (6%)
  matrix products  45 us (4%)
  between operations  15.1 us (1%)
    unnamed x24, waiting for transfers between devices  448 us
    unnamed x2, blocking collectives  115 us
    psum x1, blocking collectives, on_device(): lax.psum((segment_sums(onehot, weight_row * weight_row), segment_sums(one...  65 us
    unnamed x71, local copies, waits for them, and re-layouts  47.3 us
    all_gather x1, waiting for transfers between devices, on_device(): lax.all_gather(owned[8], 'dp', axis=0, tiled=True)  46.1 us
    all_gather x1, waiting for transfers between devices, on_device(): lax.all_gather(owned[3], 'dp', axis=0, tiled=True)  45.1 us
    all_gather x1, waiting for transfers between devices, on_device(): lax.all_gather(owned[6], 'dp', axis=0, tiled=True)  45.1 us
    all_gather x1, waiting for transfers between devices, on_device(): lax.all_gather(owned[5], 'dp', axis=0, tiled=True)  44.9 us
  transfers between devices with their start and end apart: 16, of which 14 were waited for; matrix products, arithmetic and copies ran while one was open for 9% of the time, Pallas kernels for 0%

commit v1 on v0

--- a/solution.py
+++ b/solution.py
@@ -151,7 +151,9 @@
     gathered = (
         lax.all_gather(owned[0], "dp", axis=0, tiled=True),
         lax.all_gather(owned[1], "dp", axis=0, tiled=True),
-        lax.all_gather(owned[2], "dp", axis=0, tiled=True),
+        jnp.concatenate(
+            lax.all_to_all(jnp.stack([owned[2]] * lax.axis_size("dp")), "dp", 0, 0), axis=0
+        ),
         lax.all_gather(owned[3], "dp", axis=0, tiled=True),
         lax.all_gather(owned[4], "dp", axis=0, tiled=True),
         lax.all_gather(owned[5], "dp", axis=0, tiled=True),

time: 1180 us -> 1140 us (0.966)
  waiting for transfers between devices: 748 us -> 703 us
    all_gather x1 -> x0, waiting for transfers between devices: 31.7 us -> none  [on_device(): lax.all_gather(owned[2], 'dp', axis=0, tiled=True)]
    all_gather x1, waiting for transfers between devices: 45.1 us -> 30.8 us  [on_device(): lax.all_gather(owned[3], 'dp', axis=0, tiled=True)]
    unnamed x71 -> x69, local copies, waits for them, and re-layouts: 47.3 us -> 46.7 us
    unnamed x24 -> x23, waiting for transfers between devices: 448 us -> 449 us
  transfers between devices with their start and end apart: 16 -> 16, of which waited for: 14 -> 13; matrix products, arithmetic and copies ran while one was open for 9% -> 9% of each run, Pallas kernels for 0% -> 0%
where the time goes in v1:
time: 1140 us; the launch traced here: 1130 us
  waiting for transfers between devices  703 us (62%)
  blocking collectives  182 us (16%)
  local copies, waits for them, and re-layouts  107 us (9%)
  other arithmetic  76.6 us (7%)
  matrix products  45 us (4%)
  between operations  15.1 us (1%)
    unnamed x23, waiting for transfers between devices  449 us
    unnamed x2, blocking collectives  117 us
    psum x1, blocking collectives, on_device(): lax.psum((segment_sums(onehot, weight_row * weight_row), segment_sums(one...  65 us
    unnamed x69, local copies, waits for them, and re-layouts  46.7 us
    all_gather x1, waiting for transfers between devices, on_device(): lax.all_gather(owned[8], 'dp', axis=0, tiled=True)  46.2 us
    all_gather x1, waiting for transfers between devices, on_device(): lax.all_gather(owned[5], 'dp', axis=0, tiled=True)  45.1 us
    all_gather x1, waiting for transfers between devices, on_device(): lax.all_gather(owned[6], 'dp', axis=0, tiled=True)  44.9 us
    all_gather x1, waiting for transfers between devices, on_device(): lax.all_gather(owned[10], 'dp', axis=0, tiled=True)  43.6 us
  transfers between devices with their start and end apart: 16, of which 13 were waited for; matrix products, arithmetic and copies ran while one was open for 9% of the time, Pallas kernels for 0%

profile of v1, /device:TPU:0, one launch (start us, length us, event | category | flops | bytes accessed | tf_op | source)
XLA Modules:
  0.0 1133.1 jit_solution(16901356541520015950)
XLA Ops:
  11.1 1.5 copy.40
  12.7 1.3 copy-done.2
  14.3 1.5 copy.42
  15.9 1.3 copy-done.3
  17.2 1.4 reshape_squeeze.43
  18.7 8.6 fusion.2
  27.7 13.4 %reduce = f32[299056]{0:T(1024)S(1)} reduce(f32[1,299056]{1,0:T(1,128)} %param.25, f32[]{:T(128)} %constant.110), dimensions={0}, to_apply=%param.25.reduce_sub_computation | reduce | bytes 2392452 | tf_op args[11]
  41.0 76.2 %all-reduce.16 = (bf16[16,16]{1,0:T(8,128)(2,1)S(1)}, bf16[16,16]{1,0:T(8,128)(2,1)S(1)}, bf16[16,16]{1,0:T(8,128)(2,1)S(1)}) all-reduce(bf16[16,16]{1,0:T(8,128)(2,1)S(1)} %reshape_squeeze.33, bf16[16,16]{1,0:T(8,128)(2,1)S(1)} %reshape_squeeze.37, ...), channel_id=5, replica_groups=mesh['dp'=16,'tensor'=8] {'dp'}, use_global_device_ids=true, to_apply=%region_1.0.clone | all-reduce | flops 768 | bytes 3072
  119.1 1.2 dynamic-update-slice.3
  121.0 20.0 %fusion.15 = f32[299056]{0:T(1024)} fusion(f32[11,299056]{1,0:T(8,128)} %fusion.2), kind=kLoop, calls=%fused_computation.35 | loop fusion | flops 897168 | bytes 4784896 | tf_op jit(solution)/shard_map/sub | solution.py:135
  141.0 0.9 convert_bitcast_fusion.8
  142.0 20.7 %reduce-scatter.27.cloned.1.call-done = bf16[1,128,256]{2,1,0:T(8,128)(2,1)} async-done(((bf16[16,128,256]{2,1,0:T(8,128)(2,1)}), bf16[1,128,256]{2,1,0:T(8,128)(2,1)}) %reduce-scatter.27.cloned.1.call-update) | async-done | bytes 65552
  162.8 0.9 convert_bitcast_fusion.6
  163.8 74.6 %reduce-scatter.29.cloned.1.call-done = bf16[1,128,256]{2,1,0:T(8,128)(2,1)} async-done(((bf16[16,128,256]{2,1,0:T(8,128)(2,1)}), bf16[1,128,256]{2,1,0:T(8,128)(2,1)}) %reduce-scatter.29.cloned.1.call-update) | async-done | bytes 65552
  238.3 1.5 convert_bitcast_fusion.4
  240.0 74.0 %reduce-scatter.31.cloned.1.call-done = bf16[1,128,256]{2,1,0:T(8,128)(2,1)} async-done(((bf16[16,128,256]{2,1,0:T(8,128)(2,1)}), bf16[1,128,256]{2,1,0:T(8,128)(2,1)}) %reduce-scatter.31.cloned.1.call-update) | async-done | bytes 65552
  314.0 1.5 convert_bitcast_fusion.2
  315.7 73.7 %reduce-scatter.33.cloned.1.call-done = bf16[1,16,2048]{2,1,0:T(8,128)(2,1)} async-done(((bf16[16,16,2048]{2,1,0:T(8,128)(2,1)}), bf16[1,16,2048]{2,1,0:T(8,128)(2,1)}) %reduce-scatter.33.cloned.1.call-update) | async-done | bytes 65552
  389.4 0.9 convert_bitcast_fusion
  393.4 3.8 dynamic-update-slice.4
  397.2 3.8 dynamic-update-slice.5
  400.9 3.8 dynamic-update-slice.6
  404.7 1.4 dynamic-update-slice.7
  406.0 3.8 dynamic-update-slice.8
  409.8 3.8 dynamic-update-slice.9
  413.5 1.4 dynamic-update-slice.10
  414.9 51.5 %reduce-scatter.35.cloned.1.call-done = bf16[1,128,352]{1,2,0:T(8,128)(2,1)} async-done(((bf16[16,128,352]{1,2,0:T(8,128)(2,1)}), bf16[1,128,352]{1,2,0:T(8,128)(2,1)}) %reduce-scatter.35.cloned.1.call-update) | async-done | bytes 90128
  466.4 1.0 copy.41
  467.8 75.6 %reduce-scatter.37.cloned.1.call-done = bf16[1,128,352]{1,2,0:T(8,128)(2,1)} async-done(((bf16[16,128,352]{1,2,0:T(8,128)(2,1)}), bf16[1,128,352]{1,2,0:T(8,128)(2,1)}) %reduce-scatter.37.cloned.1.call-update) | async-done | bytes 90128
  543.4 1.0 copy.43
  544.9 75.2 %reduce-scatter.39.cloned.1.call-done = bf16[1,22,2048]{2,1,0:T(8,128)(2,1)} async-done(((bf16[16,22,2048]{2,1,0:T(8,128)(2,1)}), bf16[1,22,2048]{2,1,0:T(8,128)(2,1)}) %reduce-scatter.39.cloned.1.call-update) | async-done | bytes 90128
  620.0 0.9 convert_bitcast_fusion.10
  621.1 4.4 dynamic-update-slice.11
  625.5 4.4 dynamic-update-slice.12
  629.8 4.3 dynamic-update-slice.13
  634.2 21.6 %fusion.13 = (f32[1,299056]{1,0:T(1,128)}, f32[299056]{0:T(1024)}, f32[1,299056]{1,0:T(1,128)}, f32[299056]{0:T(1024)}) fusion(f32[1,299056]{1,0:T(1,128)} %dynamic-update-slice.13, f32[1,299056]{1,0:T(1,128)} %param.27, f32[1,299056]{1,0:T(1,128)} %param.26), kind=kLoop, calls=%fused_computation.30 | loop fusion | flops 2093392 | bytes 8373568 | tf_op jit(solution)/shard_map/add | solution.py:134
  655.9 16.2 %concatenate.41 = f32[299056]{0:T(1024)} concatenate(f32[16]{0:T(128)S(1)} %bitcast.103, f32[32768]{0:T(1024)S(1)} %bitcast.93, f32[32768]{0:T(1024)S(1)} %bitcast.94, f32[32768]{0:T(1024)S(1)} %bitcast.95, f32[16]{0:T(128)S(1)} %fusion.32, f32[32768]{0:T(1024)} %bitcast.96, f32[32768]{0:T(1024)} %bitcast.97, f32[16]{0:T(128)S(1)} %bitcast.104, f32[45056]{0:T(1024)S(1)} %reshape.615, ...), dimensions={0} | concatenate | bytes 2392448 | tf_op jit(solution)/shard_map/concatenate | solution.py:132
  672.1 4.2 fusion.24
  676.3 5.7 reshape.662
  682.0 12.5 %fusion.17 = f32[11]{0:T(128)S(1)} fusion(f32[299056,1]{0,1:T(1,128)S(1)} %reshape.662, s32[299056]{0:T(1024)S(1)} %convert_add_fusion), kind=kOutput, calls=%fused_computation.37 | convolution fusion | flops 42765008 | bytes 2392492 | tf_op jit(solution)/shard_map/dot_general | solution.py:10
  694.5 5.8 reshape.660
  700.3 12.5 %fusion.16 = f32[11]{0:T(128)S(1)} fusion(f32[299056,1]{0,1:T(1,128)S(1)} %reshape.660, s32[299056]{0:T(1024)S(1)} %convert_add_fusion), kind=kOutput, calls=%fused_computation.36 | convolution fusion | flops 42765008 | bytes 2392492 | tf_op jit(solution)/shard_map/dot_general | solution.py:10
  712.8 65.0 %all-reduce.14 = (f32[11]{0:T(128)S(1)}, f32[11]{0:T(128)S(1)}) all-reduce(f32[11]{0:T(128)S(1)} %fusion.17, f32[11]{0:T(128)S(1)} %fusion.16), channel_id=1, replica_groups=mesh['dp'=16,'tensor'=8] {'dp','tensor'}, use_global_device_ids=true, to_apply=%region_12.0 | all-reduce | flops 22 | bytes 176 | tf_op jit(solution)/shard_map/psum | solution.py:136
  777.8 20.0 %fusion.7 = f32[299056]{0:T(1024)S(1)} fusion(s32[299056]{0:T(1024)S(1)} %convert_add_fusion, f32[11]{0:T(128)S(1)} %get-tuple-element.28, f32[11]{0:T(128)S(1)} %get-tuple-element.29), kind=kOutput, calls=%fused_computation.22 | convolution fusion | flops 42765020 | bytes 2392536 | tf_op jit(solution)/shard_map/dot_general | solution.py:141
  801.4 0.7 copy.46
  802.4 0.7 copy.48
  804.0 1.1 stack.3
  805.1 3.8 all-to-all-start
  809.6 6.3 reshape.618
  816.6 41.1 %all-reduce.15 = (bf16[256]{0:T(256)(128)(2,1)}, bf16[256]{0:T(256)(128)(2,1)}, bf16[256]{0:T(256)(128)(2,1)}) all-reduce(bf16[256]{0:T(256)(128)(2,1)S(1)} %dynamic-update-slice, bf16[256]{0:T(256)(128)(2,1)S(1)} %dynamic-update-slice.1, bf16[256]{0:T(256)(128)(2,1)S(1)} %dynamic-update-slice.2), channel_id=2, replica_groups=mesh['dp'=16,'tensor'=8] {'dp'}, use_global_device_ids=true, to_apply=%add | all-reduce | flops 768 | bytes 3072
  857.8 30.8 %all-gather.13.cloned.1.call-done = bf16[16,128,256]{2,1,0:T(8,128)(2,1)} async-done(((bf16[1,128,256]{2,1,0:T(8,128)(2,1)}), bf16[16,128,256]{2,1,0:T(8,128)(2,1)}) %all-gather.13.cloned.1.call-update) | async-done | bytes 1048592 | tf_op jit(solution)/shard_map/all_gather | solution.py:157
  888.6 45.1 %all-gather.15.cloned.1.call-done = bf16[16,128,256]{2,1,0:T(8,128)(2,1)} async-done(((bf16[1,128,256]{2,1,0:T(8,128)(2,1)}), bf16[16,128,256]{2,1,0:T(8,128)(2,1)}) %all-gather.15.cloned.1.call-update) | async-done | bytes 1048592 | tf_op jit(solution)/shard_map/all_gather | solution.py:159
  933.7 44.9 %all-gather.17.cloned.1.call-done = bf16[16,16,2048]{2,1,0:T(8,128)(2,1)} async-done(((bf16[1,16,2048]{2,1,0:T(8,128)(2,1)}), bf16[16,16,2048]{2,1,0:T(8,128)(2,1)}) %all-gather.17.cloned.1.call-update) | async-done | bytes 1048592 | tf_op jit(solution)/shard_map/all_gather | solution.py:160
  978.6 46.2 %all-gather.19.cloned.1.call-done = bf16[16,128,352]{1,2,0:T(8,128)(2,1)} async-done(((bf16[1,128,352]{1,2,0:T(8,128)(2,1)}), bf16[16,128,352]{1,2,0:T(8,128)(2,1)}) %all-gather.19.cloned.1.call-update) | async-done | bytes 1441808 | tf_op jit(solution)/shard_map/all_gather | solution.py:162
  1024.8 2.6 copy_bitcast_fusion.1
  1027.5 43.5 %all-gather.21.cloned.1.call-done = bf16[16,128,352]{1,2,0:T(8,128)(2,1)} async-done(((bf16[1,128,352]{1,2,0:T(8,128)(2,1)}), bf16[16,128,352]{1,2,0:T(8,128)(2,1)}) %all-gather.21.cloned.1.call-update) | async-done | bytes 1441808 | tf_op jit(solution)/shard_map/all_gather | solution.py:163
  1070.9 2.6 copy_bitcast_fusion
  1073.6 43.6 %all-gather.23.cloned.1.call-done = bf16[16,22,2048]{2,1,0:T(8,128)(2,1)} async-done(((bf16[1,22,2048]{2,1,0:T(8,128)(2,1)}), bf16[16,22,2048]{2,1,0:T(8,128)(2,1)}) %all-gather.23.cloned.1.call-update) | async-done | bytes 1441808 | tf_op jit(solution)/shard_map/all_gather | solution.py:164
  1117.2 2.4 reshape.638
  1119.6 1.0 copy.86
  1120.6 1.0 copy.87
  1122.2 1.0 copy.88
  1123.8 1.0 copy.89
  1125.4 1.0 copy.90
  (113 shorter events, 19.3 us)
Async XLA Ops:
  7.2 133.8 %reduce-scatter.25.cloned.1.call-start = ((), (), s32[]{:S(2)}) async-start(), calls=%async_computation.16 | async-start | bytes 1114112
  7.9 154.8 %reduce-scatter.27.cloned.1.call-start = ((), (), s32[]{:S(2)}) async-start(), calls=%async_computation.17 | async-start | bytes 1114112
  8.7 229.7 %reduce-scatter.29.cloned.1.call-start = ((), (), s32[]{:S(2)}) async-start(), calls=%async_computation.18 | async-start | bytes 1114112
  9.4 1.4 copy-start.1
  9.4 304.6 %reduce-scatter.31.cloned.1.call-start = ((), (), s32[]{:S(2)}) async-start(), calls=%async_computation.19 | async-start | bytes 1114112
  10.0 379.4 %reduce-scatter.33.cloned.1.call-start = ((), (), s32[]{:S(2)}) async-start(), calls=%async_computation.20 | async-start | bytes 1114112
  10.6 455.8 %reduce-scatter.35.cloned.1.call-start = ((), (), s32[]{:S(2)}) async-start(), calls=%async_computation.21 | async-start | bytes 1531904
  12.6 1.4 copy-start.2
  12.6 530.8 %reduce-scatter.37.cloned.1.call-start = ((), (), s32[]{:S(2)}) async-start(), calls=%async_computation.22 | async-start | bytes 1531904
  15.8 1.4 copy-start.3
  15.8 604.2 %reduce-scatter.39.cloned.1.call-start = ((), (), s32[]{:S(2)}) async-start(), calls=%async_computation.23 | async-start | bytes 1671168
  18.5 839.2 %all-gather.11.cloned.1.call-start = ((), (), s32[]{:S(2)}) async-start(), calls=%async_computation.9 | async-start | bytes 1114112 | tf_op jit(solution)/shard_map/all_gather | solution.py:153
  18.7 8.6 copy-start.14
  18.7 8.7 copy-start.15
  18.7 8.8 copy-start.16
  27.7 89.6 %copy-start.13 = (u32[128]{0:T(128)S(1)}, u32[128]{0:T(128)}, u32[]{:S(2)}) copy-start(u32[128]{0:T(128)} %constant.50) | copy-start | bytes 1540
  389.4 1.9 copy-start.10
  389.4 2.6 copy-start.11
  634.1 21.6 %copy-start.12 = (bf16[1,22,2048]{2,1,0:T(8,128)(2,1)S(1)}, bf16[1,22,2048]{2,1,0:T(8,128)(2,1)}, u32[]{:S(2)}) copy-start(bf16[1,22,2048]{2,1,0:T(8,128)(2,1)} %reduce-scatter.39.cloned.1.call-done) | copy-start | bytes 270340
  634.1 21.7 %copy-start.8 = (f32[16,2,8,128]{3,1,2,0:T(2,128)S(1)}, f32[16,2,8,128]{3,1,2,0:T(2,128)}, u32[]{:S(2)}) copy-start(f32[16,2,8,128]{3,1,2,0:T(2,128)} %copy.53) | copy-start | bytes 393220
  634.2 21.7 %copy-start.9 = (f32[16,2,8,128]{3,1,2,0:T(2,128)S(1)}, f32[16,2,8,128]{3,1,2,0:T(2,128)}, u32[]{:S(2)}) copy-start(f32[16,2,8,128]{3,1,2,0:T(2,128)} %copy.54) | copy-start | bytes 393220
  777.8 20.0 %copy-start = (f32[299056]{0:T(1024)S(1)}, f32[299056]{0:T(1024)}, u32[]{:S(2)}) copy-start(f32[299056]{0:T(1024)} %get-tuple-element.39) | copy-start | bytes 3588676
  798.9 89.7 %all-gather.13.cloned.1.call-start = ((), (), s32[]{:S(2)}) async-start(), calls=%async_computation.10 | async-start | bytes 1114112 | tf_op jit(solution)/shard_map/all_gather | solution.py:157
  799.6 134.1 %all-gather.15.cloned.1.call-start = ((), (), s32[]{:S(2)}) async-start(), calls=%async_computation.11 | async-start | bytes 1114112 | tf_op jit(solution)/shard_map/all_gather | solution.py:159
  800.4 178.3 %all-gather.17.cloned.1.call-start = ((), (), s32[]{:S(2)}) async-start(), calls=%async_computation.12 | async-start | bytes 1114112 | tf_op jit(solution)/shard_map/all_gather | solution.py:160
  801.1 223.7 %all-gather.19.cloned.1.call-start = ((), (), s32[]{:S(2)}) async-start(), calls=%async_computation.13 | async-start | bytes 1531904 | tf_op jit(solution)/shard_map/all_gather | solution.py:162
  802.2 268.7 %all-gather.21.cloned.1.call-start = ((), (), s32[]{:S(2)}) async-start(), calls=%async_computation.14 | async-start | bytes 1531904 | tf_op jit(solution)/shard_map/all_gather | solution.py:163
  803.2 314.0 %all-gather.23.cloned.1.call-start = ((), (), s32[]{:S(2)}) async-start(), calls=%async_computation.15 | async-start | bytes 1671168 | tf_op jit(solution)/shard_map/all_gather | solution.py:164
  805.1 52.7 %all-to-all-start = ((bf16[16,1,128,256]{3,2,1,0:T(8,128)(2,1)}), bf16[16,1,128,256]{3,2,1,0:T(8,128)(2,1)S(1)}, u32[]{:S(2)}, u32[]{:S(2)}) async-start(bf16[16,1,128,256]{3,2,1,0:T(8,128)(2,1)} %stack.3), calls=%async_computation | async-start | bytes 2097152 | tf_op jit(solution)/shard_map/all_to_all | solution.py:155
  1073.6 46.0 %copy-start.4 = (bf16[16,128,256]{2,1,0:T(8,128)(2,1)S(1)}, bf16[16,128,256]{2,1,0:T(8,128)(2,1)}, u32[]{:S(2)}) copy-start(bf16[16,128,256]{2,1,0:T(8,128)(2,1)} %all-gather.11.cloned.1.call-done) | copy-start | bytes 3145732
  1120.6 1.6 copy-start.5
  1122.2 1.6 copy-start.6
  1123.8 1.6 copy-start.7
Sparse Core Ops, SparseCore 0:
  11.2 75.6 reduce-scatter.24
  90.4 72.2 reduce-scatter.26
  166.0 72.3 reduce-scatter.28
  241.7 72.2 reduce-scatter.30
  317.1 72.2 reduce-scatter.32
  393.4 72.9 reduce-scatter.34
  470.5 72.8 reduce-scatter.36
  547.0 73.0 reduce-scatter.38
  799.0 44.6 all-gather.10
  846.4 42.1 all-gather.12
  891.6 42.0 all-gather.14
  936.5 42.0 all-gather.16
  981.6 43.1 all-gather.18
  1027.7 43.2 all-gather.20
  1073.8 43.3 all-gather.22
